TPU v7x, 32 devices: a whole 2x2x4 slice. The times are simulated.
32 devices in a mesh: grp: 8 (over z, core), dev: 4 (over y, x).
Axes of the slice: x: 2, y: 2, z: 4, core: 2. Of those that a mesh axis runs over, the one named last changes fastest.
Arguments:
- orbitals: bfloat16 [64, 256, 1024], P(('grp', 'dev')), may hold values from -6 to 6
- dens_tiles: bfloat16 [1024, 128, 128], P(('grp', 'dev')), may hold values from -0.005859375 to 0.005859375
- point_coords: float32 [3, 16384], P(None, ('grp', 'dev')), may hold values from 0 to 64
- point_weights: float32 [16384], P(('grp', 'dev')), may hold values from 0.005 to 0.05
- batch_blocks: int32 [64, 8], P(('grp', 'dev')), may hold values from 0 to 8, all different within a row
- tile_owner: int32 [2592, 1], P(('grp', 'dev')), may hold values from 0 to 3; in each aligned block of 81 rows (0 to 80, 81 to 161, ...) at most 31 rows name the same one
- tile_slot: int32 [2592], P(('grp', 'dev')), may hold values from 0 to 31
- batch_atoms: int32 [64, 4], P(('grp', 'dev')), may hold values from 0 to 3, all different within a row
- batch_weights: int32 [64, 4], P(('grp', 'dev')), may hold values from 1 to 8
- atom_grid_index: int32 [3, 32], P(None, 'grp'), may hold values from 0 to 63
Outputs:
- density: float32 [16384], P(('grp', 'dev'))
- potential: float32 [16384], P(('grp', 'dev'))
- ham_tiles: bfloat16 [1024, 128, 128], P(('grp', 'dev'))
Inputs may be any that keep to these rules, and one draw needn't show every extreme that they name: `tile_owner`: in each aligned block of 81 rows (the listed tiles of one device) no owner is named by more than 31 rows, a bound that some block reaches. `batch_blocks`: the 8 blocks of a batch are distinct. `batch_atoms`: the 4 atoms of a batch are distinct.
All inputs are finite; a program needn't handle non-finite values.
Results may differ from a plain program's by a relative error of at most 0.0056.
Values may be sent and summed in bfloat16 or wider, within the bound.
A program may use at most 64 MiB of HBM per device.

v0:
```python
import functools
import math

import jax
import jax.numpy as jnp
from jax import lax
from jax.experimental import pallas as pl
from jax.experimental.pallas import tpu as pltpu
from jax.sharding import PartitionSpec as P

TB = 128
KM = 512
GRIDN = 64
HALF = KM // 2
MESH = pl.DeviceIdType.MESH
VM = pl.BlockSpec(memory_space=pltpu.VMEM)
SM = pl.BlockSpec(memory_space=pltpu.SMEM)
ANY = pl.BlockSpec(memory_space=pl.ANY)


def modes(shape, axis):
    k = lax.broadcasted_iota(jnp.int32, shape, axis)
    return tuple(v.astype(jnp.float32) for v in (k & 7, (k >> 3) & 7, k >> 6))


def turn_trig(turns):
    angle = (turns - jnp.round(turns)) * (2.0 * math.pi)
    return jnp.cos(angle), jnp.sin(angle)


def split(value):
    high = value.astype(jnp.bfloat16)
    return high, (value - high.astype(jnp.float32)).astype(jnp.bfloat16)


def split_dot(value, table):
    rows = value.shape[0]
    high = value.astype(jnp.bfloat16)
    rest = value - high.astype(jnp.float32)
    both = jnp.concatenate([value, rest], axis=0).astype(jnp.bfloat16)
    out = jnp.dot(both, table[0], preferred_element_type=jnp.float32)
    return out[:rows] + out[rows:] + jnp.dot(high, table[1], preferred_element_type=jnp.float32)


def region_kernel(
    n, regions, orb, meta, coords, weights, dens, atoms_s, weights_s, grid_s,
    density, potential, scaled_all, meta_all, union_all, flip_all,
    table, table_t, phase, spread, turns, tiles, block, union, flip, part, part_in,
    terms, terms_in, struct, struct_in, scaled, meta_s,
    pack_sem, local_sem, send, recv, msend, mrecv, dsend, drecv, tsend, trecv, ssend, srecv, psend, precv,
    usem, fsem, *land,
):
    me = lax.axis_index("dev")
    grp = lax.axis_index("grp")
    bits = n.bit_length() - 1
    batches, points, width = orb.shape
    stored = dens.shape[0]
    blocks = union.shape[2] // TB
    held = width // TB
    packs = []
    for b in range(batches):
        for u in range(held):
            copy = pltpu.make_async_copy(
                orb.at[b, :, pl.ds(u * TB, TB)], land[0].at[b, u], pack_sem.at[b, u]
            )
            copy.start()
            packs.append(copy)
    barrier = pltpu.get_barrier_semaphore()
    for mask in range(1, n):
        pl.semaphore_signal(barrier, inc=1, device_id={"dev": me ^ mask}, device_id_type=MESH)
    for step in range(1, regions):
        pl.semaphore_signal(
            barrier, inc=1, device_id={"grp": lax.rem(grp + step, regions)}, device_id_type=MESH
        )
    for ref in land:
        for b in range(batches):
            ref[b, held] = jnp.zeros((points, TB), jnp.bfloat16)

    def clear(t, carry):
        tiles[t] = jnp.zeros((TB, TB), jnp.bfloat16)
        return carry

    lax.fori_loop(0, n * stored, clear, 0)
    for copy in packs:
        copy.wait()
    pl.semaphore_wait(barrier, n + regions - 2)

    def remote(src, dst, ssem, rsem, **where):
        return pltpu.make_async_remote_copy(
            src_ref=src, dst_ref=dst, send_sem=ssem, recv_sem=rsem,
            device_id=where, device_id_type=MESH,
        )

    def to_peers(src_of, dst_of, ssem, rsem):
        copies = []
        for mask in range(1, n):
            copy = remote(src_of(mask), dst_of(mask), ssem.at[mask], rsem.at[mask], dev=me ^ mask)
            copy.start()
            copies.append(copy)
        return copies

    def order_of(b):
        return list(range(bits)) if b % 2 == 0 else list(range(bits))[::-1]

    def landing(mask, b):
        return land[mask].at[b, pl.ds(0, held)]

    def block_copy(b, stage, mask):
        bit = 1 << order_of(b)[stage]
        got = mask ^ bit
        return remote(landing(mask, b), landing(got, b), send.at[b, got], recv.at[b, got], dev=me ^ bit)

    started = []
    metas = to_peers(lambda mask: meta, lambda mask: meta_all.at[me], msend, mrecv)
    for stage in range(bits):
        for b in range(batches):
            copy = block_copy(b, stage, 0)
            copy.start()
            started.append(copy)
    own = [
        pltpu.make_async_copy(meta, meta_all.at[me], local_sem.at[0]),
        pltpu.make_async_copy(dens, tiles.at[pl.ds(me * stored, stored)], local_sem.at[1]),
    ]
    for copy in own:
        copy.start()

    rows = 32

    def table_rows(c, carry):
        shape = (rows, batches * points)
        k = lax.broadcasted_iota(jnp.int32, shape, 0) + c * rows
        fx, fy, fz = (v.astype(jnp.float32) for v in (k & 7, (k >> 3) & 7, k >> 6))
        at = fx * coords[0:1, :] + fy * coords[1:2, :] + fz * coords[2:3, :]
        cos, sin = turn_trig(at * (1.0 / GRIDN))
        for first, wave in ((0, cos), (HALF, sin)):
            high, low = split(wave)
            at = pl.ds(pl.multiple_of(first + c * rows, rows), rows)
            table[0, at, :] = high
            table[1, at, :] = low
        return carry

    def turn_rows(c, carry):
        at = pl.ds(pl.multiple_of(c * TB, TB), TB)
        table_t[0, :, at] = table[0, at, :].T
        table_t[1, :, at] = table[1, at, :].T
        return carry

    def small_tables():
        atoms = grid_s.shape[1]
        turns[...] = jnp.zeros_like(turns)
        spread[...] = jnp.zeros_like(spread)
        fx, fy, fz = modes((1, HALF), 1)
        for a in range(atoms):
            place = [grid_s[c, a].astype(jnp.float32) for c in range(3)]
            turns[a : a + 1, :] = (fx * place[0] + fy * place[1] + fz * place[2]) * (1.0 / GRIDN)
            for b in range(batches):
                cols = slice(b * points, (b + 1) * points)
                share, total = jnp.int32(0), jnp.int32(0)
                for near in range(atoms_s.shape[1]):
                    weight = weights_s[b, near]
                    share = share + jnp.where(atoms_s[b, near] == a, weight, 0)
                    total = total + weight
                gone = [coords[c : c + 1, cols] - place[c] for c in range(3)]
                squared = gone[0] * gone[0] + gone[1] * gone[1] + gone[2] * gone[2]
                fraction = jnp.full((1, points), share.astype(jnp.float32)) / jnp.full(
                    (1, points), total.astype(jnp.float32)
                )
                spread[a : a + 1, cols] = fraction * jnp.exp(squared * (-2.0 / (GRIDN * GRIDN)))
        cos, sin = turn_trig(turns[...])
        phase[0] = cos
        phase[1] = sin

    results = {}
    density_sends = []

    def process(mask):
        e = me ^ mask
        slot = len(results) % 2
        if len(results) >= 2:
            for copy in list(results.values())[-2]:
                copy.wait()
        for b in range(batches):
            at = slice(b * points, (b + 1) * points)
            for u in range(blocks):
                index = meta_s[e, 1, b * blocks + u]
                union[slot, at, u * TB : (u + 1) * TB] = land[mask][b, index]

        total = jnp.zeros((batches * points, TB), jnp.float32)
        for c in range(0, blocks, 2):
            some = min(2, blocks - c)
            cols = slice(c * TB, (c + some) * TB)
            orbital = union[slot, :, cols]
            product = jnp.dot(union[slot], block[:, cols], preferred_element_type=jnp.float32)
            product = product * orbital.astype(jnp.float32)
            for t in range(some):
                total = total + product[:, t * TB : (t + 1) * TB]
        line = jnp.sum(total.T, axis=0, keepdims=True)
        part[mask] = jnp.broadcast_to(line, (8, batches * points))
        if mask:
            copy = remote(
                part.at[mask], part_in.at[mask], dsend.at[mask], drecv.at[mask], dev=me ^ mask
            )
            copy.start()
            density_sends.append(copy)

        def flip_block(u, carry):
            first = pl.multiple_of(u * TB, TB)
            flip[slot, pl.ds(first, TB), :] = union[slot, :, pl.ds(first, TB)].T
            return carry

        lax.fori_loop(0, blocks, flip_block, 0)
        outs = [
            pltpu.make_async_copy(union.at[slot], union_all.at[e], usem.at[mask]),
            pltpu.make_async_copy(flip.at[slot], flip_all.at[e], fsem.at[mask]),
        ]
        for copy in outs:
            copy.start()
        results[mask] = outs

    def assemble(mask):
        e = me ^ mask

        def row(i, carry):
            for j in range(blocks):
                index = meta_s[e, 0, i * blocks + j]
                block[pl.ds(pl.multiple_of(i * TB, TB), TB), j * TB : (j + 1) * TB] = tiles[index]
            return carry

        lax.fori_loop(0, blocks, row, 0)

    arrivals = []
    counts = {}
    order = [0]
    for stage in range(bits):
        for low in range(1 << stage):
            for b in range(batches):
                got = 1 << order_of(b)[stage]
                for t in range(stage):
                    if low >> t & 1:
                        got ^= 1 << order_of(b)[t]
                counts[got] = counts.get(got, 0) + 1
                arrivals.append((stage, b, got, counts[got] == batches))
                if counts[got] == batches:
                    order.append(got)
    order.append(None)
    small_tables()
    chunks = HALF // rows
    lax.fori_loop(0, chunks // 2, table_rows, 0)
    for copy in metas + own:
        copy.wait()
    to_smem = pltpu.make_async_copy(meta_all, meta_s, local_sem.at[0])
    to_smem.start()
    to_smem.wait()
    assemble(0)
    process(0)
    assemble(order[1])
    last = 0
    for stage, b, got, whole in arrivals:
        if stage != last:
            if last == 0:
                lax.fori_loop(chunks // 2, chunks, table_rows, 0)
                lax.fori_loop(0, KM // TB, turn_rows, 0)
            last = stage
        there = landing(got, b)
        bit = 1 << order_of(b)[stage]
        remote(there, there, send.at[b, got], recv.at[b, got], dev=me ^ bit).wait_recv()
        for later in range(stage + 1, bits):
            copy = block_copy(b, later, got)
            copy.start()
            started.append(copy)
        if whole:
            process(got)
            following = order[order.index(got) + 1]
            if following is not None:
                assemble(following)

    cos, sin = phase[0], phase[1]
    fx, fy, fz = modes((1, HALF), 1)
    squared = fx * fx + fy * fy + fz * fz
    near_gain = 0.1 / (1.0 + 0.1 * squared)
    far_gain = 0.03 / (1.0 + 0.1 * squared)
    rho = part[0]
    for copy in density_sends:
        copy.wait()
    for mask in range(1, n):
        rho = rho + part_in[mask]
    density[...] = rho
    source = spread[...] * (weights[...] * rho[0:1, :])
    mine = split_dot(source, table_t)
    terms[...] = mine
    copies = to_peers(lambda mask: terms, lambda mask: terms_in.at[mask], tsend, trecv)
    for mask, copy in enumerate(copies, 1):
        copy.wait()
        mine = mine + terms_in[mask]
    even, odd = mine[:, :HALF], mine[:, HALF:]
    even, odd = even * cos + odd * sin, odd * cos - even * sin
    charge = even[:, 0:1]
    total = jnp.concatenate(
        [
            jnp.sum(charge * cos, axis=0, keepdims=True),
            jnp.sum(charge * sin, axis=0, keepdims=True),
        ],
        axis=1,
    )
    total = jnp.broadcast_to(total, (8, KM))
    struct[...] = total
    copies = []
    for step in range(1, regions):
        copies.append(
            remote(
                struct, struct_in.at[step], ssend.at[step], srecv.at[step],
                grp=lax.rem(grp + step, regions),
            )
        )
        copies[-1].start()
    even, odd = even * near_gain, odd * near_gain
    coef = jnp.concatenate([even * cos - odd * sin, even * sin + odd * cos], axis=1)
    value = split_dot(coef, table)
    near = jnp.sum(value * spread[...], axis=0, keepdims=True)
    for step, copy in enumerate(copies, 1):
        copy.wait()
        total = total + struct_in[step]
    far_coef = total * jnp.concatenate([far_gain, far_gain], axis=1)
    far = split_dot(far_coef, table)
    field = near + far
    potential[...] = field
    scaled[...] = weights[...] * field
    keep = pltpu.make_async_copy(scaled, scaled_all.at[me], local_sem.at[0])
    keep.start()
    copies = to_peers(lambda mask: scaled, lambda mask: scaled_all.at[me], psend, precv)
    for outs in list(results.values())[-2:]:
        for copy in outs:
            copy.wait()
    for copy in started:
        copy.wait_send()
    for copy in copies:
        copy.wait()
    keep.wait()


def hamilton_kernel(
    meta, orb, orb_flip, scaled, density8, potential8, out, density, potential,
    total, scaled_orb, block, chosen,
):
    e = pl.program_id(0)
    me = lax.axis_index("dev")
    stored = out.shape[0]
    points, width = orb.shape[1:]
    blocks = width // TB

    @pl.when(e == 0)
    def _():
        total[...] = jnp.zeros_like(total)
        for q in range(points // TB):
            density[q : q + 1, :] = density8[0:1, q * TB : (q + 1) * TB]
            potential[q : q + 1, :] = potential8[0:1, q * TB : (q + 1) * TB]

    count = jnp.int32(0)
    for r in range(blocks * blocks):
        code = meta[e, 0, r] - me * stored
        chosen[count] = r
        count = count + ((code >= 0) & (code < stored)).astype(jnp.int32)
    column = jnp.broadcast_to(scaled[0, 0:1, :], (TB, points)).T
    for j in range(blocks):
        cols = slice(j * TB, (j + 1) * TB)
        scaled_orb[:, cols] = (column * orb[0, :, cols].astype(jnp.float32)).astype(jnp.bfloat16)
    for c in range(0, blocks, 2):
        some = min(2, blocks - c)
        product = jnp.dot(
            orb_flip[0], scaled_orb[:, c * TB : (c + some) * TB],
            preferred_element_type=jnp.float32,
        )
        for t in range(some):
            block[c + t] = product[:, t * TB : (t + 1) * TB]

    def add(q, carry):
        r = chosen[q]
        i = r // blocks
        slot = meta[e, 0, r] - me * stored
        piece = block[r - i * blocks, pl.ds(pl.multiple_of(i * TB, TB), TB), :]
        total[slot] = total[slot] + piece
        return carry

    lax.fori_loop(0, count, add, 0)

    @pl.when(e == pl.num_programs(0) - 1)
    def _():
        out[...] = total[...].astype(jnp.bfloat16)


def on_device(
    n, regions, orbitals, dens_tiles, point_coords, point_weights, batch_blocks,
    tile_owner, tile_slot, batch_atoms, batch_weights, atom_grid_index,
):
    stored = dens_tiles.shape[0]
    listed = tile_slot.shape[0]
    batches, points, width = orbitals.shape
    here = batches * points
    union = math.isqrt(listed)
    wide = union * TB
    rows = -(-atom_grid_index.shape[1] // 8) * 8
    code = tile_owner[:, 0] * stored + tile_slot
    blocks = width // TB
    hit = batch_blocks[:, None, :] == jnp.arange(union, dtype=jnp.int32)[None, :, None]
    place = blocks - jnp.sum(
        jnp.where(hit, blocks - jnp.arange(blocks, dtype=jnp.int32), 0), axis=2
    )
    meta = jnp.concatenate(
        [
            jnp.pad(code, (0, TB - listed))[None],
            jnp.pad(place.reshape(-1), (0, TB - batches * union))[None],
            jnp.zeros((6, TB), jnp.int32),
        ]
    )
    f32, i32, bf16 = jnp.float32, jnp.int32, jnp.bfloat16
    S = jax.ShapeDtypeStruct
    dma = pltpu.SemaphoreType.DMA
    V = pltpu.VMEM
    density, potential, scaled_all, meta_all, union_all, flip_all = pl.pallas_call(
        functools.partial(region_kernel, n, regions),
        out_shape=(
            S((8, here), f32),
            S((8, here), f32),
            S((n, 8, here), f32),
            S((n, 8, TB), i32),
            S((n, here, wide), bf16),
            S((n, wide, here), bf16),
        ),
        in_specs=[ANY, VM, VM, VM, ANY, SM, SM, SM],
        out_specs=(VM, VM, VM, ANY, ANY, ANY),
        scratch_shapes=[
            V((2, KM, here), bf16),
            V((2, here, KM), bf16),
            V((2, rows, HALF), f32),
            V((rows, here), f32),
            V((rows, HALF), f32),
            V((n * stored, TB, TB), bf16),
            V((wide, wide), bf16),
            V((2, here, wide), bf16),
            V((2, wide, here), bf16),
            V((n, 8, here), f32),
            V((n, 8, here), f32),
            V((rows, KM), f32),
            V((n, rows, KM), f32),
            V((8, KM), f32),
            V((regions, 8, KM), f32),
            V((8, here), f32),
            pltpu.SMEM((n, 8, TB), i32),
            dma((batches, blocks)),
            dma((2,)),
            dma((batches, n)), dma((batches, n)),
            dma((n,)), dma((n,)), dma((n,)), dma((n,)), dma((n,)), dma((n,)),
            dma((regions,)), dma((regions,)), dma((n,)), dma((n,)), dma((n,)), dma((n,)),
            *[V((batches, blocks + 1, points, TB), bf16) for _ in range(n)],
        ],
        compiler_params=pltpu.CompilerParams(collective_id=0, has_side_effects=True),
        name="region",
    )(
        orbitals, meta, point_coords, point_weights.reshape(1, here), dens_tiles,
        batch_atoms, batch_weights, atom_grid_index,
    )
    ham_tiles, density, potential = pl.pallas_call(
        hamilton_kernel,
        grid=(n,),
        out_shape=(
            S((stored, TB, TB), bf16), S((here // TB, TB), f32), S((here // TB, TB), f32),
        ),
        in_specs=[
            SM,
            pl.BlockSpec((1, here, wide), lambda e: (e, 0, 0)),
            pl.BlockSpec((1, wide, here), lambda e: (e, 0, 0)),
            pl.BlockSpec((1, 8, here), lambda e: (e, 0, 0)),
            VM,
            VM,
        ],
        out_specs=(VM, VM, VM),
        scratch_shapes=[
            V((stored, TB, TB), f32),
            V((here, wide), bf16),
            V((union, wide, TB), f32),
            pltpu.SMEM((listed + 1,), i32),
        ],
        name="hamilton",
    )(meta_all, union_all, flip_all, scaled_all, density, potential)
    return density.reshape(-1), potential.reshape(-1), ham_tiles


def solution(mesh):
    body = functools.partial(on_device, mesh.shape["dev"], mesh.shape["grp"])
    in_specs = (
        P(("grp", "dev"), None, None),
        P(("grp", "dev"), None, None),
        P(None, ("grp", "dev")),
        P(("grp", "dev")),
        P(("grp", "dev"), None),
        P(("grp", "dev"), None),
        P(("grp", "dev")),
        P(("grp", "dev"), None),
        P(("grp", "dev"), None),
        P(None, "grp"),
    )
    out_specs = (P(("grp", "dev")), P(("grp", "dev")), P(("grp", "dev"), None, None))
    return jax.shard_map(body, mesh=mesh, in_specs=in_specs, out_specs=out_specs, check_vma=False)
```

profile of v0, /device:TPU:0, one launch (start us, length us, event | category | flops | bytes accessed | tf_op | source)
XLA Modules:
  0.0 76.2 jit_solution(1384053174643852923)
XLA Ops:
  0.6 0.7 bitcast_add_fusion
  1.3 0.1 pad.12.clone
  1.4 0.8 %select_reduce_fusion = s32[2,9]{1,0:T(2,128)S(1)} fusion(s32[8]{0:T(128)S(1)} %iota_subtract_fusion, s32[2,8]{1,0:T(2,128)} %param.14), kind=kLoop, calls=%fused_computation | loop fusion | flops 414 | bytes 168 | tf_op jit(solution)/shard_map/reduce_sum | solution.py:405
  2.2 0.1 sub.12
  2.3 0.7 add_add_fusion.meta
  2.9 59.7 %region.1 = (f32[8,512]{1,0:T(8,128)}, f32[8,512]{1,0:T(8,128)}, f32[4,8,512]{2,1,0:T(8,128)}, s32[4,8,128]{2,1,0:T(8,128)}, bf16[4,512,1152]{2,1,0:T(8,128)(2,1)}, /*index=5*/bf16[4,1152,512]{2,1,0:T(8,128)(2,1)}) custom-call(bf16[2,256,1024]{2,1,0:T(8,128)(2,1)} %orb.1, s32[8,128]{1,0:T(8,128)} %add_add_fusion.meta, f32[3,512]{1,0:T(4,128)} %coords.1, ...), custom_call_target="tpu_custom_call" | custom-call | tf_op jit(solution)/shard_map/region/pallas_call | solution.py:419
  62.6 13.6 %hamilton.1 = (bf16[32,128,128]{2,1,0:T(8,128)(2,1)}, f32[4,128]{1,0:T(4,128)}, f32[4,128]{1,0:T(4,128)}) custom-call(s32[4,8,128]{2,1,0:T(8,128)} %get-tuple-element.12.meta, bf16[4,512,1152]{2,1,0:T(8,128)(2,1)} %get-tuple-element.13.orb, bf16[4,1152,512]{2,1,0:T(8,128)(2,1)} %get-tuple-element.14.orb_flip, f32[4,8,512]{2,1,0:T(8,128)} %get-tuple-element.15.scaled, ...), custom_call_target="tpu_custom_call" | custom-call | tf_op jit(solution)/shard_map/hamilton/pallas_call | solution.py:462
  (4 shorter events, 0.0 us)
where the time goes:
time: 76 us; the launch traced here: 76.2 us
  Pallas kernels  73.3 us (96%)
  other arithmetic  2.11 us (3%)
    pallas_call x1, Pallas kernels, on_device(): pl.pallas_call(functools.partial(region_kernel, n, regions), out_shape=(S...  59.7 us
    pallas_call x1, Pallas kernels, on_device(): pl.pallas_call(hamilton_kernel, grid=(n,), out_shape=(S((stored, TB, TB),...  13.6 us

commit v1 on v0

v1 whole, which is shorter than its diff:
```python
import functools
import math

import jax
import jax.numpy as jnp
from jax import lax
from jax.experimental import pallas as pl
from jax.experimental.pallas import tpu as pltpu
from jax.sharding import PartitionSpec as P

TB = 128
KM = 512
GRIDN = 64
FXY = 64
FZ = KM // 2 // FXY
WAVES = 2 * FZ
MESH = pl.DeviceIdType.MESH
VM = pl.BlockSpec(memory_space=pltpu.VMEM)
SM = pl.BlockSpec(memory_space=pltpu.SMEM)
ANY = pl.BlockSpec(memory_space=pl.ANY)
f32, i32, bf16 = jnp.float32, jnp.int32, jnp.bfloat16


def turn_trig(turns):
    angle = (turns - jnp.round(turns)) * (2.0 * math.pi)
    return jnp.cos(angle), jnp.sin(angle)


def stack_split(value):
    high = value.astype(bf16)
    rest = (value - high.astype(f32)).astype(bf16)
    return jnp.concatenate([high, rest], axis=0)


def table_dot(both, high, low, turned):
    rows = both.shape[0] // 2
    dims = (((1,), (1 if turned else 0,)), ((), ()))
    out = lax.dot_general(both, high, dims, preferred_element_type=f32)
    fine = lax.dot_general(both[:rows], low, dims, preferred_element_type=f32)
    return out[:rows] + out[rows:] + fine


def lane_modes(shape):
    lane = lax.broadcasted_iota(i32, shape, 1)
    fx = (lane & 7).astype(f32)
    fy = ((lane >> 3) & 7).astype(f32)
    return lane, fx, fy


def half_turn(value, first, second):
    lane = lax.broadcasted_iota(i32, value.shape, 1)
    return pltpu.roll(value, FXY, 1) * jnp.where(lane < FXY, first, second)


def region_kernel(
    n, regions, parts, listed, near, orb, meta, coords, weights, dens, grid_s,
    density, potential, scaled, meta_all, land, flip,
    meta_v, meta_s, coords_all, weights_all, tiles, block,
    t1h, t1l, t2, spread, wrow, far, lhs_far, waves, part, part_in,
    macc, moments, moments_in, near_acc, qacc, charge, charge_in,
    pack_sem, local_sem, send, recv, fsend, frecv, wsend, wrecv,
    dsend, drecv, tsend, trecv, qsend, qrecv, ready,
):
    me = lax.axis_index("dev")
    grp = lax.axis_index("grp")
    bits = n.bit_length() - 1
    batches, points, width = orb.shape
    here = batches * points
    held = width // TB
    union = math.isqrt(listed)
    stored = dens.shape[0]
    atoms = grid_s.shape[1]
    rows = spread.shape[0]
    piece = points // parts
    lanes = charge.shape[2]
    block_at = listed
    atom_at = block_at + batches * held
    weight_at = atom_at + batches * near

    packs = []
    for b in range(batches):
        for u in range(held):
            copy = pltpu.make_async_copy(
                orb.at[b, :, pl.ds(u * TB, TB)], land.at[0, b, u], pack_sem.at[b, u]
            )
            copy.start()
            packs.append(copy)
    own = [pltpu.make_async_copy(dens, tiles.at[pl.ds(0, stored)], local_sem.at[0])]
    own[0].start()
    barrier = pltpu.get_barrier_semaphore()
    for mask in range(1, n):
        pl.semaphore_signal(barrier, inc=1, device_id={"dev": me ^ mask}, device_id_type=MESH)
    for step in range(1, regions):
        pl.semaphore_signal(
            barrier, inc=1, device_id={"grp": lax.rem(grp + step, regions)}, device_id_type=MESH
        )
    tiles[stored] = jnp.zeros((TB, TB), bf16)
    macc[...] = jnp.zeros_like(macc)
    qacc[...] = jnp.zeros_like(qacc)
    for copy in packs:
        copy.wait()
    pl.semaphore_wait(barrier, n + regions - 2)

    def remote(src, dst, ssem, rsem, **where):
        return pltpu.make_async_remote_copy(
            src_ref=src, dst_ref=dst, send_sem=ssem, recv_sem=rsem,
            device_id=where, device_id_type=MESH,
        )

    def order_of(b):
        return list(range(bits)) if b % 2 == 0 else list(range(bits))[::-1]

    def landing(mask, b, c):
        return land.at[mask, b, :, pl.ds(c * piece, piece), :]

    def orb_copy(b, stage, mask, c):
        bit = 1 << order_of(b)[stage]
        got = mask ^ bit
        return remote(
            landing(mask, b, c), landing(got, b, c), send.at[b, c, got], recv.at[b, c, got],
            dev=me ^ bit,
        )

    started = []
    feats = []
    pairs = ((meta, meta_v), (coords, coords_all), (weights, weights_all))
    for mask in range(1, n):
        for k, (src, dst) in enumerate(pairs):
            copy = remote(src, dst.at[me], fsend.at[k, mask], frecv.at[k, mask], dev=me ^ mask)
            copy.start()
            feats.append(copy)
    for stage in range(bits):
        for b in range(batches):
            for c in range(parts):
                copy = orb_copy(b, stage, 0, c)
                copy.start()
                started.append(copy)
    for k, (src, dst) in enumerate(pairs, 1):
        copy = pltpu.make_async_copy(src, dst.at[me], local_sem.at[k])
        copy.start()
        own.append(copy)
    for mask in range(1, n):
        pl.semaphore_signal(ready, inc=1, device_id={"dev": me ^ mask}, device_id_type=MESH)

    shape = (rows, TB)
    lane, fx, fy = lane_modes(shape)
    row = lax.broadcasted_iota(i32, shape, 0)
    place = []
    for c in range(3):
        at = jnp.zeros(shape, f32)
        for a in range(atoms):
            at = jnp.where(row == a, grid_s[c, a].astype(f32), at)
        place.append(at)
    for z in range(FZ):
        turns = (fx * place[0] + fy * place[1] + place[2] * float(z)) * (1.0 / GRIDN)
        cos, sin = turn_trig(turns)
        gain = 0.03 / (1.0 + 0.1 * (fx * fx + fy * fy + float(z * z)))
        wave = jnp.where(lane < FXY, cos, sin) * gain
        waves[grp, z] = jnp.where(row < atoms, wave, 0.0)
    wave_copies = []
    for step in range(1, regions):
        copy = remote(
            waves.at[grp], waves.at[grp], wsend.at[step], wrecv.at[step],
            grp=lax.rem(grp + step, regions),
        )
        copy.start()
        wave_copies.append(copy)

    for copy in feats + own:
        copy.wait()
    codes = meta_v[...]
    at = lax.broadcasted_iota(i32, codes.shape, 2)
    local = codes - me * stored
    mine = (local >= 0) & (local < stored)
    meta_v[...] = jnp.where(at < listed, jnp.where(mine, local, stored), codes)
    moved = [
        pltpu.make_async_copy(meta_v, meta_s, local_sem.at[0]),
        pltpu.make_async_copy(meta_v, meta_all, local_sem.at[1]),
    ]
    for copy in moved:
        copy.start()

    def mask_cols(mask, first, count):
        return pl.ds(pl.multiple_of(mask * here + first, TB), count)

    def tables(mask, carry):
        e = me ^ mask
        cols = mask_cols(mask, 0, here)
        step = lax.broadcasted_iota(i32, (8, here), 0)
        where = coords_all[e]
        first = []
        for c in range(2):
            turns = step.astype(f32) * where[c : c + 1, :] * (1.0 / GRIDN)
            first.append(turn_trig(turns))
        (cx, sx), (cy, sy) = first
        for y in range(0, 8, 2):
            cos, sin = [], []
            for q in (y, y + 1):
                cq, sq = cy[q : q + 1, :], sy[q : q + 1, :]
                cos.append(cx * cq - sx * sq)
                sin.append(sx * cq + cx * sq)
            for base, wave in ((0, cos), (FXY, sin)):
                wave = jnp.concatenate(wave, axis=0)
                high = wave.astype(bf16)
                t1h[base + y * 8 : base + y * 8 + 16, cols] = high
                t1l[base + y * 8 : base + y * 8 + 16, cols] = (wave - high.astype(f32)).astype(bf16)
        step = lax.broadcasted_iota(i32, (WAVES, here), 0)
        times = jnp.where(step < FZ, step, step - FZ).astype(f32)
        cz, sz = turn_trig(times * where[2:3, :] * (1.0 / GRIDN))
        t2[:, cols] = jnp.where(step < FZ, cz, sz)
        wrow[:, cols] = weights_all[e]
        row = lax.broadcasted_iota(i32, (rows, points), 0)
        for b in range(batches):
            total = jnp.int32(0)
            for k in range(near):
                total = total + meta_s[e, 0, weight_at + b * near + k]
            share = jnp.zeros((rows, points), i32)
            spot = [jnp.zeros((rows, points), f32) for c in range(3)]
            for a in range(atoms):
                part_of = jnp.int32(0)
                for k in range(near):
                    weight = meta_s[e, 0, weight_at + b * near + k]
                    part_of = part_of + jnp.where(
                        meta_s[e, 0, atom_at + b * near + k] == a, weight, 0
                    )
                share = jnp.where(row == a, part_of, share)
                for c in range(3):
                    spot[c] = jnp.where(row == a, grid_s[c, a].astype(f32), spot[c])
            squared = jnp.zeros((rows, points), f32)
            for c in range(3):
                gone = where[c : c + 1, b * points : (b + 1) * points] - spot[c]
                squared = squared + gone * gone
            fraction = share.astype(f32) / jnp.full((rows, points), total.astype(f32))
            spread[:, mask_cols(mask, b * points, points)] = fraction * jnp.exp(
                squared * (-2.0 / (GRIDN * GRIDN))
            )
        return carry

    def far_rows():
        for z in range(FZ):
            for g in range(regions):
                cs = waves[g, z]
                for j, value in ((z, cs), (FZ + z, half_turn(cs, 1.0, -1.0))):
                    high = value.astype(bf16)
                    first = (j * regions + g) * rows
                    lhs_far[0, first : first + rows, :] = value
        return None

    def far_cols(q, carry):
        cols = pl.ds(pl.multiple_of(q * 2 * TB, 2 * TB), 2 * TB)
        high, low = t1h[:, cols], t1l[:, cols]
        every = regions * rows
        total = jnp.zeros((every, 2 * TB), f32)
        for j in range(WAVES):
            value = lhs_far[0, j * every : (j + 1) * every, :]
            out = table_dot(stack_split(value), high, low, False)
            total = total + out * t2[j : j + 1, cols]
        far[:, cols] = total
        return carry

    def assemble(mask, b):
        e = me ^ mask

        def block_row(i, carry):
            first = meta_s[e, 0, block_at + b * held + i] * union
            for j in range(held):
                index = meta_s[e, 0, first + meta_s[e, 0, block_at + b * held + j]]
                block[b, pl.ds(pl.multiple_of(i * TB, TB), TB), j * TB : (j + 1) * TB] = tiles[index]
            return carry

        lax.fori_loop(0, held, block_row, 0)

    def process(mask, b, c):
        at = slice(c * piece, (c + 1) * piece)
        cols = slice(mask * here + b * points + c * piece, mask * here + b * points + (c + 1) * piece)
        orbital = [land[mask, b, u, at, :] for u in range(held)]
        lhs = jnp.concatenate(orbital, axis=1)
        total = jnp.zeros((piece, TB), f32)
        for v in range(0, held, 2):
            some = min(2, held - v)
            product = jnp.dot(lhs, block[b, :, v * TB : (v + some) * TB], preferred_element_type=f32)
            for t in range(some):
                total = total + product[:, t * TB : (t + 1) * TB] * orbital[v + t].astype(f32)
        line = jnp.sum(total.T, axis=0, keepdims=True)
        part[mask, :, b * points + c * piece : b * points + (c + 1) * piece] = line
        source = spread[:, cols] * (wrow[:, cols] * line)
        folded = source[:, 0:TB]
        for q in range(TB, piece, TB):
            folded = folded + source[:, q : q + TB]
        qacc[...] = qacc[...] + folded
        waved = jnp.concatenate([source * t2[j : j + 1, cols] for j in range(WAVES)], axis=0)
        macc[...] = macc[...] + table_dot(stack_split(waved), t1h[:, cols], t1l[:, cols], True)

    def turn(mask, b, c):
        at = slice(c * piece, (c + 1) * piece)
        for u in range(held):
            flip[mask, b, u * TB : (u + 1) * TB, at] = land[mask, b, u, at, :].T

    density_sends = []

    def send_density(mask):
        if mask:
            copy = remote(
                part.at[mask], part_in.at[mask], dsend.at[mask], drecv.at[mask], dev=me ^ mask
            )
            copy.start()
            density_sends.append(copy)

    rounds = [(None, [0] * batches)]
    for stage in range(bits):
        for low in range(1 << stage):
            masks = []
            for b in range(batches):
                got = 1 << order_of(b)[stage]
                for t in range(stage):
                    if low >> t & 1:
                        got ^= 1 << order_of(b)[t]
                masks.append(got)
            rounds.append((stage, masks))
    done = {}
    for copy in moved:
        copy.wait()
    lax.fori_loop(0, n, tables, 0)
    for number, (stage, masks) in enumerate(rounds):
        last = number == len(rounds) - 1
        for b in range(batches):
            assemble(masks[b], b)
        if last:
            for copy in wave_copies:
                copy.wait()
            far_rows()
            lax.fori_loop(0, n * here // (2 * TB), far_cols, 0)
        for c in range(parts):
            for b in range(batches):
                mask = masks[b]
                if stage is not None:
                    there = landing(mask, b, c)
                    bit = 1 << order_of(b)[stage]
                    remote(
                        there, there, send.at[b, c, mask], recv.at[b, c, mask], dev=me ^ bit
                    ).wait_recv()
                    for later in range(stage + 1, bits):
                        copy = orb_copy(b, later, mask, c)
                        copy.start()
                        started.append(copy)
                process(mask, b, c)
                if not last:
                    turn(mask, b, c)
        for mask in masks:
            done[mask] = done.get(mask, 0) + 1
            if done[mask] == batches and not last:
                send_density(mask)

    column = jnp.sum(qacc[...], axis=1, keepdims=True)
    shape = (rows, lanes)
    lane = lax.broadcasted_iota(i32, shape, 1)
    row = lax.broadcasted_iota(i32, shape, 0)
    spot = jnp.where(lane == grp * rows + row, jnp.broadcast_to(column, shape), 0.0)
    mine = jnp.sum(spot, axis=0, keepdims=True)
    charge[0] = mine
    pl.semaphore_wait(ready, n - 1)
    charge_copies = []
    for step in reversed(range(regions)):
        for mask in reversed(range(n)):
            if step or mask:
                slot = step * n + mask
                copy = remote(
                    charge.at[0], charge_in.at[slot], qsend.at[slot], qrecv.at[slot],
                    grp=lax.rem(grp + step, regions), dev=me ^ mask,
                )
                copy.start()
                charge_copies.append(copy)
    waved = macc[...]
    sums = []
    for z in range(FZ):
        cos = waved[z * rows : (z + 1) * rows]
        sin = waved[(FZ + z) * rows : (FZ + z + 1) * rows]
        sums.append(cos + half_turn(sin, -1.0, 1.0))
        moments[z] = sums[z]
    moment_copies = []
    for mask in range(1, n):
        copy = remote(
            moments, moments_in.at[mask], tsend.at[mask], trecv.at[mask], dev=me ^ mask
        )
        copy.start()
        moment_copies.append(copy)
    for mask in dict.fromkeys(rounds[-1][1]):
        send_density(mask)
    for copy in moment_copies:
        copy.wait()
    lane, fx, fy = lane_modes((rows, TB))
    first, second = [], []
    for z in range(FZ):
        for mask in range(1, n):
            sums[z] = sums[z] + moments_in[mask, z]
        gain = 0.1 / (1.0 + 0.1 * (fx * fx + fy * fy + float(z * z)))
        value = sums[z] * gain
        first.append(value)
        second.append(half_turn(value, 1.0, -1.0))
    both = stack_split(jnp.concatenate(first + second, axis=0))

    def near_cols(first, count):
        cols = pl.ds(first, count)
        out = table_dot(both, t1h[:, cols], t1l[:, cols], False)
        total = jnp.zeros((rows, count), f32)
        for j in range(WAVES):
            total = total + out[j * rows : (j + 1) * rows] * t2[j : j + 1, cols]
        near_acc[:, cols] = jnp.sum(total * spread[:, cols], axis=0, keepdims=True)

    for q in range(0, n * here, here):
        near_cols(q, here)
    for c in range(parts):
        for b in range(batches):
            turn(rounds[-1][1][b], b, c)
    for copy in density_sends:
        copy.wait()
    rho = part[0]
    for mask in range(1, n):
        rho = rho + part_in[mask]
    density[...] = rho
    for copy in started:
        copy.wait_send()

    for copy in charge_copies:
        copy.wait()
    total = mine
    for slot in range(1, n * regions):
        total = total + charge_in[slot]
    every = regions * rows
    shape = (every, lanes)
    lane = lax.broadcasted_iota(i32, shape, 1)
    row = lax.broadcasted_iota(i32, shape, 0)
    spot = jnp.where(lane == row, jnp.broadcast_to(total, shape), 0.0)
    column = jnp.sum(spot, axis=1, keepdims=True)
    for q in range(0, n * here, here):
        cols = slice(q, q + here)
        field = near_acc[:, cols] + jnp.sum(far[:, cols] * column, axis=0, keepdims=True)
        if q == 0:
            potential[...] = field
        scaled[q // here] = wrow[:, cols] * field


def hamilton_kernel(
    meta, land, flip, scaled, density8, potential8, out, density, potential, totals,
    *, listed,
):
    n, batches, held, points = land.shape[:4]
    union = math.isqrt(listed)
    stored = out.shape[0]
    block_at = listed
    me = lax.axis_index("dev")
    banks = totals.shape[0]
    for q in range(density.shape[0]):
        density[q : q + 1, :] = density8[0:1, q * TB : (q + 1) * TB]
        potential[q : q + 1, :] = potential8[0:1, q * TB : (q + 1) * TB]

    def clear(t, carry):
        for k in range(banks):
            totals[k, t] = jnp.zeros((TB, TB), f32)
        return carry

    lax.fori_loop(0, stored + 1, clear, 0)

    def one(item, carry):
        mask = item // batches
        b = item - mask * batches
        e = me ^ mask
        line = scaled[mask, :, pl.ds(pl.multiple_of(b * points, TB), points)]
        column = jnp.broadcast_to(line, (TB, points)).T
        right = [
            (column * land[mask, b, j].astype(f32)).astype(bf16) for j in range(held)
        ]
        left = flip[mask, b]
        spots = [meta[e, 0, block_at + b * held + i] for i in range(held)]
        turn = 0
        for j in range(0, held, 2):
            some = min(2, held - j)
            product = jnp.dot(
                left, jnp.concatenate(right[j : j + some], axis=1), preferred_element_type=f32
            )
            for i in range(held):
                for t in range(some):
                    slot = meta[e, 0, spots[i] * union + spots[j + t]]
                    tile = product[i * TB : (i + 1) * TB, t * TB : (t + 1) * TB]
                    totals[turn % banks, slot] = totals[turn % banks, slot] + tile
                    turn += 1
        return carry

    lax.fori_loop(0, n * batches, one, 0)

    def finish(t, carry):
        value = totals[0, t]
        for k in range(1, banks):
            value = value + totals[k, t]
        out[t] = value.astype(bf16)
        return carry

    lax.fori_loop(0, stored, finish, 0)


def on_device(
    n, regions, orbitals, dens_tiles, point_coords, point_weights, batch_blocks,
    tile_owner, tile_slot, batch_atoms, batch_weights, atom_grid_index,
):
    stored = dens_tiles.shape[0]
    listed = tile_slot.shape[0]
    batches, points, width = orbitals.shape
    near = batch_atoms.shape[1]
    here = batches * points
    held = width // TB
    atoms = atom_grid_index.shape[1]
    rows = -(-atoms // 8) * 8
    parts = 2
    banks = 2
    code = tile_owner[:, 0] * stored + tile_slot
    facts = [code, batch_blocks.reshape(-1), batch_atoms.reshape(-1), batch_weights.reshape(-1)]
    count = sum(fact.shape[0] for fact in facts)
    wide = -(-count // TB) * TB
    meta = jnp.pad(jnp.concatenate(facts), (0, wide - count))[None]
    lanes = -(-regions * rows // TB) * TB
    kept = 4 * n * batches * points * width + 64 * n * here + (1 << 20)
    grant = (62 << 20) - kept
    S = jax.ShapeDtypeStruct
    dma = pltpu.SemaphoreType.DMA
    V = pltpu.VMEM
    density, potential, scaled, meta_all, land, flip = pl.pallas_call(
        functools.partial(region_kernel, n, regions, parts, listed, near),
        out_shape=(
            V((1, here), f32),
            V((1, here), f32),
            V((n, 1, here), f32),
            S((n, 1, wide), i32),
            V((n, batches, held, points, TB), bf16),
            V((n, batches, width, points), bf16),
        ),
        in_specs=[ANY, VM, VM, VM, ANY, SM],
        out_specs=(VM, VM, VM, ANY, VM, VM),
        scratch_shapes=[
            V((n, 1, wide), i32),
            pltpu.SMEM((n, 1, wide), i32),
            V((n, 3, here), f32),
            V((n, 1, here), f32),
            V((stored + 1, TB, TB), bf16),
            V((batches, width, width), bf16),
            V((2 * FXY, n * here), bf16),
            V((2 * FXY, n * here), bf16),
            V((WAVES, n * here), f32),
            V((rows, n * here), f32),
            V((1, n * here), f32),
            V((regions * rows, n * here), f32),
            V((1, WAVES * regions * rows, TB), f32),
            V((regions, FZ, rows, TB), f32),
            V((n, 1, here), f32),
            V((n, 1, here), f32),
            V((WAVES * rows, TB), f32),
            V((FZ, rows, TB), f32),
            V((n, FZ, rows, TB), f32),
            V((1, n * here), f32),
            V((rows, TB), f32),
            V((1, 1, lanes), f32),
            V((n * regions, 1, lanes), f32),
            dma((batches, held)),
            dma((4,)),
            dma((batches, parts, n)), dma((batches, parts, n)),
            dma((3, n)), dma((3, n)),
            dma((regions,)), dma((regions,)),
            dma((n,)), dma((n,)), dma((n,)), dma((n,)),
            dma((n * regions,)), dma((n * regions,)),
            pltpu.SemaphoreType.REGULAR,
        ],
        compiler_params=pltpu.CompilerParams(
            collective_id=0, has_side_effects=True, vmem_limit_bytes=grant
        ),
        name="region",
    )(
        orbitals, meta, point_coords, point_weights.reshape(1, here), dens_tiles, atom_grid_index,
    )
    density, potential, scaled, land, flip = [
        pltpu.with_memory_space_constraint(value, pltpu.VMEM)
        for value in (density, potential, scaled, land, flip)
    ]
    ham_tiles, density, potential = pl.pallas_call(
        functools.partial(hamilton_kernel, listed=listed),
        out_shape=(
            S((stored, TB, TB), bf16), S((here // TB, TB), f32), S((here // TB, TB), f32),
        ),
        in_specs=[SM, VM, VM, VM, VM, VM],
        out_specs=(VM, VM, VM),
        scratch_shapes=[V((banks, stored + 1, TB, TB), f32)],
        compiler_params=pltpu.CompilerParams(vmem_limit_bytes=grant),
        name="hamilton",
    )(meta_all, land, flip, scaled, density, potential)
    return density.reshape(-1), potential.reshape(-1), ham_tiles


def solution(mesh):
    body = functools.partial(on_device, mesh.shape["dev"], mesh.shape["grp"])
    in_specs = (
        P(("grp", "dev"), None, None),
        P(("grp", "dev"), None, None),
        P(None, ("grp", "dev")),
        P(("grp", "dev")),
        P(("grp", "dev"), None),
        P(("grp", "dev"), None),
        P(("grp", "dev")),
        P(("grp", "dev"), None),
        P(("grp", "dev"), None),
        P(None, "grp"),
    )
    out_specs = (P(("grp", "dev")), P(("grp", "dev")), P(("grp", "dev"), None, None))
    return jax.shard_map(body, mesh=mesh, in_specs=in_specs, out_specs=out_specs, check_vma=False)
```

time: 76 us -> 65.1 us (0.86)
  Pallas kernels: 73.3 us -> 60.6 us
  local copies, waits for them, and re-layouts: 0.17 us -> 2.79 us
  other arithmetic: 2.11 us -> 0.75 us
    pallas_call x2, Pallas kernels: 73.3 us -> 60.6 us  [the longest x1 50 us: on_device(): pl.pallas_call(functools.partial(region_kernel, n, regions, parts, listed...]
    reshape x0 -> x3, local copies, waits for them, and re-layouts: none -> 2.28 us  [the longest x1 0.76 us: on_device(): batch_blocks.reshape(-1)]
    reduce_sum x1 -> x0, other arithmetic: 0.76 us -> none  [on_device(): jnp.sum(jnp.where(hit, blocks - jnp.arange(blocks, dtype=jnp.int32), 0),...]
where the time goes in v1:
time: 65.1 us; the launch traced here: 64.8 us
  Pallas kernels  60.6 us (93%)
  local copies, waits for them, and re-layouts  2.79 us (4%)
  other arithmetic  0.75 us (1%)
    pallas_call x1, Pallas kernels, on_device(): pl.pallas_call(functools.partial(region_kernel, n, regions, parts, listed...  50 us
    pallas_call x1, Pallas kernels, on_device(): pl.pallas_call(functools.partial(hamilton_kernel, listed=listed), out_sha...  10.6 us

profile of v1, /device:TPU:0, one launch (start us, length us, event | category | flops | bytes accessed | tf_op | source)
XLA Modules:
  0.0 64.8 jit_solution(8476591070558820371)
XLA Ops:
  0.6 0.8 %reshape.26 = s32[16]{0:T(128)S(1)} reshape(s32[2,8]{1,0:T(2,128)} %param.14) | data formatting | bytes 128 | tf_op jit(solution)/shard_map/reshape | solution.py:516
  1.4 0.7 %bitcast_add_fusion = s32[81]{0:T(128)S(1)} fusion(s32[81]{0:T(128)} %param.16, s32[81,1]{0,1:T(1,128)} %param.15), kind=kLoop, calls=%fused_computation.1 | loop fusion | flops 162 | bytes 972 | tf_op jit(solution)/shard_map/add | solution.py:515
  2.1 0.8 %reshape.27 = s32[8]{0:T(128)S(1)} reshape(s32[2,4]{1,0:T(2,128)} %param.17) | data formatting | bytes 64 | tf_op jit(solution)/shard_map/reshape | solution.py:516
  2.8 0.8 %reshape.28 = s32[8]{0:T(128)S(1)} reshape(s32[2,4]{1,0:T(2,128)} %param.18) | data formatting | bytes 64 | tf_op jit(solution)/shard_map/reshape | solution.py:516
  3.6 0.1 pad_add_fusion
  3.7 0.5 pad_bitcast_fusion.meta
  4.2 50.0 %region.1 = (f32[1,512]{1,0:T(1,128)S(1)}, f32[1,512]{1,0:T(1,128)S(1)}, f32[4,1,512]{2,1,0:T(1,128)S(1)}, s32[4,1,128]{2,1,0:T(1,128)}, bf16[4,2,8,256,128]{4,3...) custom-call(bf16[2,256,1024]{2,1,0:T(8,128)(2,1)} %orb.1, s32[1,128]{1,0:T(1,128)} %pad_bitcast_fusion.meta, ...), custom_call_target="tpu_custom_call" | custom-call | tf_op jit(solution)/shard_map/region/pallas_call | solution.py:526
  54.1 10.6 %hamilton.1 = (bf16[32,128,128]{2,1,0:T(8,128)(2,1)}, f32[4,128]{1,0:T(4,128)}, f32[4,128]{1,0:T(4,128)}) custom-call(s32[4,1,128]{2,1,0:T(1,128)} %get-tuple-element.12.meta, bf16[4,2,8,256,128]{4,3,2,1,0:T(8,128)(2,1)S(1)} %get-tuple-element.13.land, bf16[4,2,1024,256]{3,2,1,0:T(8,128)(2,1)S(1)} %get-tuple-element.14.flip, ...), custom_call_target="tpu_custom_call" | custom-call | tf_op jit(solution)/shard_map/hamilton/pallas_call | solution.py:582

commit v2 on v1

--- a/solution.py
+++ b/solution.py
@@ -53,9 +53,10 @@
 
 
 def region_kernel(
-    n, regions, parts, listed, near, orb, meta, coords, weights, dens, grid_s,
+    n, regions, parts, orb, owner, slot, blocks, batch_atoms, batch_weights, coords, weights,
+    dens, grid_s,
     density, potential, scaled, meta_all, land, flip,
-    meta_v, meta_s, coords_all, weights_all, tiles, block,
+    facts, meta_v, meta_s, coords_all, weights_all, tiles, block,
     t1h, t1l, t2, spread, wrow, far, lhs_far, waves, part, part_in,
     macc, moments, moments_in, near_acc, qacc, charge, charge_in,
     pack_sem, local_sem, send, recv, fsend, frecv, wsend, wrecv,
@@ -67,15 +68,15 @@
     batches, points, width = orb.shape
     here = batches * points
     held = width // TB
-    union = math.isqrt(listed)
     stored = dens.shape[0]
     atoms = grid_s.shape[1]
     rows = spread.shape[0]
     piece = points // parts
     lanes = charge.shape[2]
-    block_at = listed
-    atom_at = block_at + batches * held
-    weight_at = atom_at + batches * near
+    listed = owner.shape[1]
+    near = batch_atoms.shape[1]
+    union = math.isqrt(listed)
+    block_at, atom_at, weight_at = 1, 1 + batches, 1 + 2 * batches
 
     packs = []
     for b in range(batches):
@@ -94,6 +95,11 @@
         pl.semaphore_signal(
             barrier, inc=1, device_id={"grp": lax.rem(grp + step, regions)}, device_id_type=MESH
         )
+    facts[...] = jnp.zeros_like(facts)
+    facts[0:1, 0:listed] = owner[...] * stored + slot[...]
+    facts[block_at : block_at + batches, 0:held] = blocks[...]
+    facts[atom_at : atom_at + batches, 0:near] = batch_atoms[...]
+    facts[weight_at : weight_at + batches, 0:near] = batch_weights[...]
     tiles[stored] = jnp.zeros((TB, TB), bf16)
     macc[...] = jnp.zeros_like(macc)
     qacc[...] = jnp.zeros_like(qacc)
@@ -123,7 +129,7 @@
 
     started = []
     feats = []
-    pairs = ((meta, meta_v), (coords, coords_all), (weights, weights_all))
+    pairs = ((facts, meta_v), (coords, coords_all), (weights, weights_all))
     for mask in range(1, n):
         for k, (src, dst) in enumerate(pairs):
             copy = remote(src, dst.at[me], fsend.at[k, mask], frecv.at[k, mask], dev=me ^ mask)
@@ -169,14 +175,11 @@
     for copy in feats + own:
         copy.wait()
     codes = meta_v[...]
-    at = lax.broadcasted_iota(i32, codes.shape, 2)
+    at = lax.broadcasted_iota(i32, codes.shape, 1)
     local = codes - me * stored
     mine = (local >= 0) & (local < stored)
-    meta_v[...] = jnp.where(at < listed, jnp.where(mine, local, stored), codes)
-    moved = [
-        pltpu.make_async_copy(meta_v, meta_s, local_sem.at[0]),
-        pltpu.make_async_copy(meta_v, meta_all, local_sem.at[1]),
-    ]
+    meta_all[...] = jnp.where(at == 0, jnp.where(mine, local, stored), codes)
+    moved = [pltpu.make_async_copy(meta_all, meta_s, local_sem.at[0])]
     for copy in moved:
         copy.start()
 
@@ -213,15 +216,15 @@
         for b in range(batches):
             total = jnp.int32(0)
             for k in range(near):
-                total = total + meta_s[e, 0, weight_at + b * near + k]
+                total = total + meta_s[e, weight_at + b, k]
             share = jnp.zeros((rows, points), i32)
             spot = [jnp.zeros((rows, points), f32) for c in range(3)]
             for a in range(atoms):
                 part_of = jnp.int32(0)
                 for k in range(near):
-                    weight = meta_s[e, 0, weight_at + b * near + k]
+                    weight = meta_s[e, weight_at + b, k]
                     part_of = part_of + jnp.where(
-                        meta_s[e, 0, atom_at + b * near + k] == a, weight, 0
+                        meta_s[e, atom_at + b, k] == a, weight, 0
                     )
                 share = jnp.where(row == a, part_of, share)
                 for c in range(3):
@@ -241,7 +244,6 @@
             for g in range(regions):
                 cs = waves[g, z]
                 for j, value in ((z, cs), (FZ + z, half_turn(cs, 1.0, -1.0))):
-                    high = value.astype(bf16)
                     first = (j * regions + g) * rows
                     lhs_far[0, first : first + rows, :] = value
         return None
@@ -262,9 +264,9 @@
         e = me ^ mask
 
         def block_row(i, carry):
-            first = meta_s[e, 0, block_at + b * held + i] * union
+            first = meta_s[e, block_at + b, i] * union
             for j in range(held):
-                index = meta_s[e, 0, first + meta_s[e, 0, block_at + b * held + j]]
+                index = meta_s[e, 0, first + meta_s[e, block_at + b, j]]
                 block[b, pl.ds(pl.multiple_of(i * TB, TB), TB), j * TB : (j + 1) * TB] = tiles[index]
             return carry
 
@@ -441,61 +443,77 @@
 
 
 def hamilton_kernel(
-    meta, land, flip, scaled, density8, potential8, out, density, potential, totals,
-    *, listed,
+    union, meta_v, land, flip, scaled, density8, potential8, out, density, potential,
+    meta, result, meta_sem, out_sem, *scratch,
 ):
     n, batches, held, points = land.shape[:4]
-    union = math.isqrt(listed)
     stored = out.shape[0]
-    block_at = listed
     me = lax.axis_index("dev")
-    banks = totals.shape[0]
+    rights, totals = scratch[:batches], scratch[batches:]
+    banks = len(totals)
+    fetch = pltpu.make_async_copy(meta_v, meta, meta_sem)
+    fetch.start()
     for q in range(density.shape[0]):
         density[q : q + 1, :] = density8[0:1, q * TB : (q + 1) * TB]
         potential[q : q + 1, :] = potential8[0:1, q * TB : (q + 1) * TB]
 
     def clear(t, carry):
-        for k in range(banks):
-            totals[k, t] = jnp.zeros((TB, TB), f32)
+        for total in totals:
+            total[t] = jnp.zeros((TB, TB), f32)
         return carry
 
+    def prepare(mask, b):
+        line = scaled[mask, :, b * points : (b + 1) * points]
+        column = jnp.broadcast_to(line, (TB, points)).T
+        for j in range(held):
+            rights[b][:, j * TB : (j + 1) * TB] = (column * land[mask, b, j].astype(f32)).astype(bf16)
+
+    def one(mask, carry):
+        e = me ^ mask
+        for b in range(batches):
+            if b + 1 < batches:
+                prepare(mask, b + 1)
+            else:
+                prepare(jnp.minimum(mask + 1, n - 1), 0)
+            left = flip[mask, b]
+            spots = [meta[e, 1 + b, i] for i in range(held)]
+            turn = 0
+            for j in range(0, held, 2):
+                some = min(2, held - j)
+                product = jnp.dot(
+                    left, rights[b][:, j * TB : (j + some) * TB], preferred_element_type=f32
+                )
+                for i in range(held):
+                    for t in range(some):
+                        slot = meta[e, 0, spots[i] * union + spots[j + t]]
+                        tile = product[i * TB : (i + 1) * TB, t * TB : (t + 1) * TB]
+                        total = totals[turn % banks]
+                        total[slot] = total[slot] + tile
+                        turn += 1
+        return carry
+
     lax.fori_loop(0, stored + 1, clear, 0)
-
-    def one(item, carry):
-        mask = item // batches
-        b = item - mask * batches
-        e = me ^ mask
-        line = scaled[mask, :, pl.ds(pl.multiple_of(b * points, TB), points)]
-        column = jnp.broadcast_to(line, (TB, points)).T
-        right = [
-            (column * land[mask, b, j].astype(f32)).astype(bf16) for j in range(held)
-        ]
-        left = flip[mask, b]
-        spots = [meta[e, 0, block_at + b * held + i] for i in range(held)]
-        turn = 0
-        for j in range(0, held, 2):
-            some = min(2, held - j)
-            product = jnp.dot(
-                left, jnp.concatenate(right[j : j + some], axis=1), preferred_element_type=f32
-            )
-            for i in range(held):
-                for t in range(some):
-                    slot = meta[e, 0, spots[i] * union + spots[j + t]]
-                    tile = product[i * TB : (i + 1) * TB, t * TB : (t + 1) * TB]
-                    totals[turn % banks, slot] = totals[turn % banks, slot] + tile
-                    turn += 1
-        return carry
-
-    lax.fori_loop(0, n * batches, one, 0)
-
-    def finish(t, carry):
-        value = totals[0, t]
-        for k in range(1, banks):
-            value = value + totals[k, t]
-        out[t] = value.astype(bf16)
-        return carry
-
-    lax.fori_loop(0, stored, finish, 0)
+    prepare(0, 0)
+    fetch.wait()
+    lax.fori_loop(0, n, one, 0, unroll=2)
+
+    group = math.gcd(stored, 8)
+    copies = []
+    for first in range(0, stored, group):
+        def finish(t, carry):
+            value = totals[0][t]
+            for total in totals[1:]:
+                value = value + total[t]
+            result[t] = value.astype(bf16)
+            return carry
+
+        lax.fori_loop(first, first + group, finish, 0)
+        at = pl.ds(first, group)
+        copy = pltpu.make_async_copy(result.at[at], out.at[at], out_sem.at[first // group])
+        copy.start()
+        copies.append(copy)
+    for copy in copies:
+        copy.wait()
 
 
 def on_device(
@@ -505,18 +523,13 @@
     stored = dens_tiles.shape[0]
     listed = tile_slot.shape[0]
     batches, points, width = orbitals.shape
-    near = batch_atoms.shape[1]
     here = batches * points
     held = width // TB
     atoms = atom_grid_index.shape[1]
     rows = -(-atoms // 8) * 8
     parts = 2
     banks = 2
-    code = tile_owner[:, 0] * stored + tile_slot
-    facts = [code, batch_blocks.reshape(-1), batch_atoms.reshape(-1), batch_weights.reshape(-1)]
-    count = sum(fact.shape[0] for fact in facts)
-    wide = -(-count // TB) * TB
-    meta = jnp.pad(jnp.concatenate(facts), (0, wide - count))[None]
+    table = (-(-(1 + 3 * batches) // 8) * 8, -(-listed // TB) * TB)
     lanes = -(-regions * rows // TB) * TB
     kept = 4 * n * batches * points * width + 64 * n * here + (1 << 20)
     grant = (62 << 20) - kept
@@ -524,20 +537,21 @@
     dma = pltpu.SemaphoreType.DMA
     V = pltpu.VMEM
     density, potential, scaled, meta_all, land, flip = pl.pallas_call(
-        functools.partial(region_kernel, n, regions, parts, listed, near),
+        functools.partial(region_kernel, n, regions, parts),
         out_shape=(
             V((1, here), f32),
             V((1, here), f32),
             V((n, 1, here), f32),
-            S((n, 1, wide), i32),
+            V((n, *table), i32),
             V((n, batches, held, points, TB), bf16),
             V((n, batches, width, points), bf16),
         ),
-        in_specs=[ANY, VM, VM, VM, ANY, SM],
-        out_specs=(VM, VM, VM, ANY, VM, VM),
+        in_specs=[ANY, VM, VM, VM, VM, VM, VM, VM, ANY, SM],
+        out_specs=(VM, VM, VM, VM, VM, VM),
         scratch_shapes=[
-            V((n, 1, wide), i32),
-            pltpu.SMEM((n, 1, wide), i32),
+            V(table, i32),
+            V((n, *table), i32),
+            pltpu.SMEM((n, *table), i32),
             V((n, 3, here), f32),
             V((n, 1, here), f32),
             V((stored + 1, TB, TB), bf16),
@@ -573,20 +587,29 @@
         ),
         name="region",
     )(
-        orbitals, meta, point_coords, point_weights.reshape(1, here), dens_tiles, atom_grid_index,
+        orbitals, tile_owner.reshape(1, listed), tile_slot.reshape(1, listed), batch_blocks,
+        batch_atoms, batch_weights, point_coords, point_weights.reshape(1, here), dens_tiles,
+        atom_grid_index,
     )
-    density, potential, scaled, land, flip = [
+    density, potential, scaled, meta_all, land, flip = [
         pltpu.with_memory_space_constraint(value, pltpu.VMEM)
-        for value in (density, potential, scaled, land, flip)
+        for value in (density, potential, scaled, meta_all, land, flip)
     ]
     ham_tiles, density, potential = pl.pallas_call(
-        functools.partial(hamilton_kernel, listed=listed),
+        functools.partial(hamilton_kernel, math.isqrt(listed)),
         out_shape=(
             S((stored, TB, TB), bf16), S((here // TB, TB), f32), S((here // TB, TB), f32),
         ),
-        in_specs=[SM, VM, VM, VM, VM, VM],
-        out_specs=(VM, VM, VM),
-        scratch_shapes=[V((banks, stored + 1, TB, TB), f32)],
+        in_specs=[VM, VM, VM, VM, VM, VM],
+        out_specs=(ANY, VM, VM),
+        scratch_shapes=[
+            pltpu.SMEM((n, *table), i32),
+            V((stored, TB, TB), bf16),
+            dma,
+            dma((stored // math.gcd(stored, 8),)),
+            *[V((points, width), bf16) for _ in range(batches)],
+            *[V((stored + 1, TB, TB), f32) for _ in range(banks)],
+        ],
         compiler_params=pltpu.CompilerParams(vmem_limit_bytes=grant),
         name="hamilton",
     )(meta_all, land, flip, scaled, density, potential)

time: 65.1 us -> 60.1 us (0.923)
  local copies, waits for them, and re-layouts: 2.79 us -> 0 us
  Pallas kernels: 60.6 us -> 59.1 us
  other arithmetic: 0.75 us -> 0 us
    reshape x3 -> x0, local copies, waits for them, and re-layouts: 2.28 us -> none  [the longest x1 0.76 us: on_device(): batch_blocks.reshape(-1)]
    pallas_call x2, Pallas kernels: 60.6 us -> 59.1 us  [the longest x1 50.1 us: on_device(): pl.pallas_call(functools.partial(region_kernel, n, regions, parts), out_s...]
    add x1 -> x0, other arithmetic: 0.67 us -> none  [on_device(): code = tile_owner[:, 0] * stored + tile_slot]
where the time goes in v2:
time: 60.1 us; the launch traced here: 59.9 us
  Pallas kernels  59.1 us (98%)
  between operations  0.8 us (1%)
    pallas_call x1, Pallas kernels, on_device(): pl.pallas_call(functools.partial(region_kernel, n, regions, parts), out_s...  50.1 us
    pallas_call x1, Pallas kernels, on_device(): pl.pallas_call(functools.partial(hamilton_kernel, math.isqrt(listed)), ou...  8.96 us

profile of v2, /device:TPU:0, one launch (start us, length us, event | category | flops | bytes accessed | tf_op | source)
XLA Modules:
  0.0 59.9 jit_solution(15620907565302593911)
XLA Ops:
  0.6 50.1 %region.1 = (f32[1,512]{1,0:T(1,128)S(1)}, f32[1,512]{1,0:T(1,128)S(1)}, f32[4,1,512]{2,1,0:T(1,128)S(1)}, s32[4,8,128]{2,1,0:T(8,128)S(1)}, bf16[4,2,8,256,128]...) custom-call(bf16[2,256,1024]{2,1,0:T(8,128)(2,1)} %orb.1, s32[1,81]{1,0:T(1,128)} %bitcast.6, ...), custom_call_target="tpu_custom_call" | custom-call | tf_op jit(solution)/shard_map/region/pallas_call | solution.py:539
  50.8 9.0 %hamilton.1 = (bf16[32,128,128]{2,1,0:T(8,128)(2,1)}, f32[4,128]{1,0:T(4,128)}, f32[4,128]{1,0:T(4,128)}) custom-call(s32[4,8,128]{2,1,0:T(8,128)S(1)} %get-tuple-element.12.meta_v, bf16[4,2,8,256,128]{4,3,2,1,0:T(8,128)(2,1)S(1)} %get-tuple-element.13.land, bf16[4,2,1024,256]{3,2,1,0:T(8,128)(2,1)S(1)} %get-tuple-element.14.flip, ...), custom_call_target="tpu_custom_call" | custom-call | tf_op jit(solution)/shard_map/hamilton/pallas_call | solution.py:598

commit v3 on v2

--- a/solution.py
+++ b/solution.py
@@ -78,6 +78,13 @@
     union = math.isqrt(listed)
     block_at, atom_at, weight_at = 1, 1 + batches, 1 + 2 * batches
 
+    barrier = pltpu.get_barrier_semaphore()
+    for mask in range(1, n):
+        pl.semaphore_signal(barrier, inc=1, device_id={"dev": me ^ mask}, device_id_type=MESH)
+    for step in range(1, regions):
+        pl.semaphore_signal(
+            barrier, inc=1, device_id={"grp": lax.rem(grp + step, regions)}, device_id_type=MESH
+        )
     packs = []
     for b in range(batches):
         for u in range(held):
@@ -88,13 +95,6 @@
             packs.append(copy)
     own = [pltpu.make_async_copy(dens, tiles.at[pl.ds(0, stored)], local_sem.at[0])]
     own[0].start()
-    barrier = pltpu.get_barrier_semaphore()
-    for mask in range(1, n):
-        pl.semaphore_signal(barrier, inc=1, device_id={"dev": me ^ mask}, device_id_type=MESH)
-    for step in range(1, regions):
-        pl.semaphore_signal(
-            barrier, inc=1, device_id={"grp": lax.rem(grp + step, regions)}, device_id_type=MESH
-        )
     facts[...] = jnp.zeros_like(facts)
     facts[0:1, 0:listed] = owner[...] * stored + slot[...]
     facts[block_at : block_at + batches, 0:held] = blocks[...]
@@ -290,6 +290,9 @@
         for q in range(TB, piece, TB):
             folded = folded + source[:, q : q + TB]
         qacc[...] = qacc[...] + folded
+        return source, cols
+
+    def gather(source, cols):
         waved = jnp.concatenate([source * t2[j : j + 1, cols] for j in range(WAVES)], axis=0)
         macc[...] = macc[...] + table_dot(stack_split(waved), t1h[:, cols], t1l[:, cols], True)
 
@@ -345,9 +348,13 @@
                         copy = orb_copy(b, later, mask, c)
                         copy.start()
                         started.append(copy)
-                process(mask, b, c)
-                if not last:
-                    turn(mask, b, c)
+            sources = [process(masks[b], b, c) for b in range(batches)]
+            if not (last and c == parts - 1):
+                for source in sources:
+                    gather(*source)
+            if not last:
+                for b in range(batches):
+                    turn(masks[b], b, c)
         for mask in masks:
             done[mask] = done.get(mask, 0) + 1
             if done[mask] == batches and not last:
@@ -372,6 +379,8 @@
                 )
                 copy.start()
                 charge_copies.append(copy)
+    for source in sources:
+        gather(*source)
     waved = macc[...]
     sums = []
     for z in range(FZ):
@@ -388,6 +397,9 @@
         moment_copies.append(copy)
     for mask in dict.fromkeys(rounds[-1][1]):
         send_density(mask)
+    for c in range(parts):
+        for b in range(batches):
+            turn(rounds[-1][1][b], b, c)
     for copy in moment_copies:
         copy.wait()
     lane, fx, fy = lane_modes((rows, TB))
@@ -411,9 +423,6 @@
 
     for q in range(0, n * here, here):
         near_cols(q, here)
-    for c in range(parts):
-        for b in range(batches):
-            turn(rounds[-1][1][b], b, c)
     for copy in density_sends:
         copy.wait()
     rho = part[0]

time: 60.1 us -> 59.8 us (level)
  no operation moved by 1% of the time
where the time goes in v3:
time: 59.8 us; the launch traced here: 59.6 us
  Pallas kernels  58.8 us (98%)
  between operations  0.8 us (1%)
    pallas_call x1, Pallas kernels, on_device(): pl.pallas_call(functools.partial(region_kernel, n, regions, parts), out_s...  49.9 us
    pallas_call x1, Pallas kernels, on_device(): pl.pallas_call(functools.partial(hamilton_kernel, math.isqrt(listed)), ou...  8.96 us

profile of v3, /device:TPU:0, one launch (start us, length us, event | category | flops | bytes accessed | tf_op | source)
XLA Modules:
  0.0 59.6 jit_solution(14515926473641357263)
XLA Ops:
  0.6 49.9 %region.1 = (f32[1,512]{1,0:T(1,128)S(1)}, f32[1,512]{1,0:T(1,128)S(1)}, f32[4,1,512]{2,1,0:T(1,128)S(1)}, s32[4,8,128]{2,1,0:T(8,128)S(1)}, bf16[4,2,8,256,128]...) custom-call(bf16[2,256,1024]{2,1,0:T(8,128)(2,1)} %orb.1, s32[1,81]{1,0:T(1,128)} %bitcast.6, ...), custom_call_target="tpu_custom_call" | custom-call | tf_op jit(solution)/shard_map/region/pallas_call | solution.py:548
  50.5 9.0 %hamilton.1 = (bf16[32,128,128]{2,1,0:T(8,128)(2,1)}, f32[4,128]{1,0:T(4,128)}, f32[4,128]{1,0:T(4,128)}) custom-call(s32[4,8,128]{2,1,0:T(8,128)S(1)} %get-tuple-element.12.meta_v, bf16[4,2,8,256,128]{4,3,2,1,0:T(8,128)(2,1)S(1)} %get-tuple-element.13.land, bf16[4,2,1024,256]{3,2,1,0:T(8,128)(2,1)S(1)} %get-tuple-element.14.flip, ...), custom_call_target="tpu_custom_call" | custom-call | tf_op jit(solution)/shard_map/hamilton/pallas_call | solution.py:607

commit v4 on v3

--- a/solution.py
+++ b/solution.py
@@ -489,22 +489,25 @@
             turn = 0
             for j in range(0, held, 2):
                 some = min(2, held - j)
-                product = jnp.dot(
-                    left, rights[b][:, j * TB : (j + some) * TB], preferred_element_type=f32
-                )
-                for i in range(held):
-                    for t in range(some):
-                        slot = meta[e, 0, spots[i] * union + spots[j + t]]
-                        tile = product[i * TB : (i + 1) * TB, t * TB : (t + 1) * TB]
-                        total = totals[turn % banks]
-                        total[slot] = total[slot] + tile
-                        turn += 1
+                right = rights[b][:, j * TB : (j + some) * TB]
+                for first in range(0, held, 2):
+                    product = jnp.dot(
+                        left[first * TB : (first + 2) * TB], right, preferred_element_type=f32
+                    )
+                    for i in range(first, min(first + 2, held)):
+                        for t in range(some):
+                            slot = meta[e, 0, spots[i] * union + spots[j + t]]
+                            at = slice((i - first) * TB, (i - first + 1) * TB)
+                            tile = product[at, t * TB : (t + 1) * TB]
+                            total = totals[turn % banks]
+                            total[slot] = total[slot] + tile
+                            turn += 1
         return carry
 
     lax.fori_loop(0, stored + 1, clear, 0)
     prepare(0, 0)
     fetch.wait()
-    lax.fori_loop(0, n, one, 0, unroll=2)
+    lax.fori_loop(0, n, one, 0, unroll=4)
 
     group = math.gcd(stored, 8)
     copies = []

time: 59.8 us -> 58.8 us (0.983)
  Pallas kernels: 58.8 us -> 57.8 us
    pallas_call x1, Pallas kernels: 8.96 us -> 7.95 us  [on_device(): pl.pallas_call(functools.partial(hamilton_kernel, math.isqrt(listed)), ou...]
where the time goes in v4:
time: 58.8 us; the launch traced here: 58.6 us
  Pallas kernels  57.8 us (98%)
  between operations  0.8 us (1%)
    pallas_call x1, Pallas kernels, on_device(): pl.pallas_call(functools.partial(region_kernel, n, regions, parts), out_s...  49.9 us
    pallas_call x1, Pallas kernels, on_device(): pl.pallas_call(functools.partial(hamilton_kernel, math.isqrt(listed)), ou...  7.95 us

profile of v4, /device:TPU:0, one launch (start us, length us, event | category | flops | bytes accessed | tf_op | source)
XLA Modules:
  0.0 58.6 jit_solution(4723846164327847811)
XLA Ops:
  0.6 49.9 %region.1 = (f32[1,512]{1,0:T(1,128)S(1)}, f32[1,512]{1,0:T(1,128)S(1)}, f32[4,1,512]{2,1,0:T(1,128)S(1)}, s32[4,8,128]{2,1,0:T(8,128)S(1)}, bf16[4,2,8,256,128]...) custom-call(bf16[2,256,1024]{2,1,0:T(8,128)(2,1)} %orb.1, s32[1,81]{1,0:T(1,128)} %bitcast.6, ...), custom_call_target="tpu_custom_call" | custom-call | tf_op jit(solution)/shard_map/region/pallas_call | solution.py:551
  50.5 8.0 %hamilton.1 = (bf16[32,128,128]{2,1,0:T(8,128)(2,1)}, f32[4,128]{1,0:T(4,128)}, f32[4,128]{1,0:T(4,128)}) custom-call(s32[4,8,128]{2,1,0:T(8,128)S(1)} %get-tuple-element.12.meta_v, bf16[4,2,8,256,128]{4,3,2,1,0:T(8,128)(2,1)S(1)} %get-tuple-element.13.land, bf16[4,2,1024,256]{3,2,1,0:T(8,128)(2,1)S(1)} %get-tuple-element.14.flip, ...), custom_call_target="tpu_custom_call" | custom-call | tf_op jit(solution)/shard_map/hamilton/pallas_call | solution.py:610
